TPU v7x, 512 devices: a whole 4x8x8 slice. The times are simulated.
512 devices in a mesh: grp: 16 (over z, x_hi), blk: 32 (over x_lo, y, core).
Axes of the slice: x: 4 (x_hi: 2, x_lo: 2; x = x_hi * 2 + x_lo), y: 8, z: 8, core: 2. Of those that a mesh axis runs over, the one named last changes fastest.
Arguments:
- ao_ints: bfloat16 [128, 1504, 1504], P('grp', 'blk'), may hold values from -6 to 6
- v_coeff: bfloat16 [1504, 1344], P(None, 'blk'), may hold values from -0.15625 to 0.15625
- batch_start: int32 [16], replicated, may hold values from 0 to 1496, as said below
- owner_map: int32 [32], replicated, may hold values from 0 to 31, each once
Outputs:
- slab: bfloat16 [128, 1344, 1344], P(None, 'blk', 'grp')
Inputs may be any that keep to these rules, and one draw needn't show every extreme that they name: `batch_start`: distinct multiples of 8; one entry is 0 and one is 1496. `owner_map`: each block number appears once.
All inputs are finite; a program needn't handle non-finite values.
Results may differ from a plain program's by a relative error of at most 0.0049.
Values may be sent and summed in bfloat16 or wider, within the bound.
No kernel may reach another device: no remote copies, remote signals or barrier semaphores. Data moves between devices by JAX's collectives and lax.ppermute only.
A program may use at most 64 MiB of HBM per device.

v0:
```python
import jax
import jax.numpy as jnp
from jax import lax
from jax.sharding import PartitionSpec as P


def in_blocks(x, dim, size):
    before, after = (x.shape[:dim], x.shape[dim + 1 :])
    return jnp.moveaxis(x.reshape(*before, size, -1, *after), dim, 0)


def edges_of(length, count):
    unit = 8 if length >= 8 * count else 1
    return [length // unit * k // count * unit for k in range(1, count)]


def joined_along(pieces, dim):
    pieces = jnp.moveaxis(pieces, 0, dim)
    lengths = pieces.shape
    return pieces.reshape(*lengths[:dim], lengths[dim] * lengths[dim + 1], *lengths[dim + 2 :])


def several_exchanges(x, axis, pieces, split_dim, concat_dim):
    blocks = in_blocks(x, split_dim, lax.axis_size(axis))
    split_at = max(range(1, max(2, blocks.ndim - 1)), key=lambda d: blocks.shape[d])
    gathered = []
    for section in jnp.split(blocks, edges_of(blocks.shape[split_at], pieces), axis=split_at):
        if section.size:
            gathered.append(lax.all_to_all(section, axis, split_axis=0, concat_axis=0, tiled=True))
    return joined_along(jnp.concatenate(gathered, axis=split_at), concat_dim)


def local(ao_ints, v_coeff, batch_start, owner_map):
    sig_rows, lam_rows, ao_count = ao_ints.shape
    ints_flat = ao_ints.reshape(sig_rows * lam_rows, ao_count)
    v_whole = lax.all_gather(v_coeff, "blk", axis=1, tiled=True)
    half_done = jnp.dot(ints_flat, v_whole, preferred_element_type=jnp.float32).astype(jnp.bfloat16)
    half_done = half_done.reshape(sig_rows, lam_rows, -1)
    owned_rows = lax.all_to_all(half_done, "blk", split_axis=2, concat_axis=1, tiled=True)
    third_done = lax.dot_general(
        owned_rows, v_whole, (((1,), (0,)), ((), ())), preferred_element_type=jnp.float32
    ).astype(jnp.bfloat16)
    a_local = third_done.shape[1]
    block_count = owner_map.shape[0]
    block_width = third_done.shape[2] // block_count
    blocked = third_done.reshape(sig_rows, a_local, block_count, block_width)
    ordered = jnp.take(blocked, owner_map, axis=2).reshape(
        sig_rows, a_local, block_count * block_width
    )
    group_count = batch_start.shape[0]
    group_ids = jnp.arange(group_count, dtype=jnp.int32)
    rank = jnp.sum((batch_start[None, :] < batch_start[:, None]).astype(jnp.int32), axis=1)
    source = jnp.sum(
        group_ids[None, :] * (rank[None, :] == group_ids[:, None]).astype(jnp.int32), axis=1
    )
    received = several_exchanges(ordered, "grp", 2, 2, 0)
    item_count = received.shape[1]
    own_width = received.shape[2]
    grouped = received.reshape(group_count, sig_rows, item_count, own_width)
    return jnp.take(grouped, source, axis=0).reshape(group_count * sig_rows, item_count, own_width)


def solution(mesh):
    return jax.shard_map(
        local,
        mesh=mesh,
        in_specs=(P("grp", "blk", None), P(None, "blk"), P(), P()),
        out_specs=P(None, "blk", "grp"),
        check_vma=False,
    )
```

profile of v0, /device:TPU:8, one launch (start us, length us, event | category | flops | bytes accessed | tf_op | source)
XLA Modules:
  0.0 247.0 jit_solution(10376196617440628879)
XLA Ops:
  6.5 0.0 all-gather.3.cloned.1.call-start
  6.5 0.7 all-gather.3.cloned.1.call-update
  7.3 1.6 copy.37
  8.9 0.5 reshape.43
  9.4 73.7 %all-gather.3.cloned.1.call-done = bf16[32,42,1504]{2,1,0:T(8,128)(2,1)} async-done(((bf16[1,42,1504]{2,1,0:T(8,128)(2,1)}), bf16[32,42,1504]{2,1,0:T(8,128)(2,1)}) %all-gather.3.cloned.1.call-update) | async-done | bytes 4042768 | tf_op jit(solution)/shard_map/all_gather | solution.py:36
  83.1 7.5 %reshape.64 = bf16[1344,1504]{1,0:T(8,128)(2,1)} reshape(bf16[32,42,1504]{2,1,0:T(8,128)(2,1)} %all-gather.3.cloned.1.call-done) | data formatting | bytes 8085504
  90.6 5.5 %convolution_convert_fusion.1 = bf16[376,1344]{0,1:T(8,128)(2,1)} fusion(bf16[376,1504]{1,0:T(8,128)(2,1)S(1)} %reshape.43, bf16[1344,1504]{1,0:T(8,128)(2,1)} %reshape.64), kind=kOutput, calls=%fused_computation.3 | convolution fusion | flops 1520580096 | bytes 6184448 | tf_op jit(solution)/shard_map/dot_general | solution.py:37
  96.1 3.8 %reshape.66 = bf16[8,47,1344]{1,0,2:T(8,128)(2,1)S(1)} reshape(bf16[376,1344]{0,1:T(8,128)(2,1)} %convolution_convert_fusion.1) | data formatting | bytes 2021376 | tf_op jit(solution)/shard_map/reshape | solution.py:38
  99.9 4.9 %reshape.70 = bf16[32,2,7896]{2,1,0:T(2,128)(2,1)} reshape(bf16[1344,8,47]{2,1,0:T(8,128)(2,1)S(1)} %bitcast.31) | data formatting | bytes 2021376
  104.8 0.0 copy-start
  104.8 7.7 %all-to-all-start = ((bf16[32,2,7896]{2,1,0:T(2,128)(2,1)}), bf16[32,2,7896]{2,1,0:T(2,128)(2,1)}, u32[]{:S(2)}, u32[]{:S(2)}) async-start(bf16[32,2,7896]{2,1,0:T(2,128)(2,1)} %reshape.70), calls=%async_computation | async-start | bytes 2031616 | tf_op jit(solution)/shard_map/all_to_all | solution.py:39
  112.6 0.0 copy-done
  112.6 0.1 broadcast_in_dim.40
  112.7 0.1 broadcast_in_dim.41
  112.8 0.1 broadcast_in_dim.42
  112.9 7.5 %reshape.65 = bf16[1344,1504,1]{1,0,2:T(8,128)(2,1)} reshape(bf16[32,42,1504]{2,1,0:T(8,128)(2,1)} %all-gather.3.cloned.1.call-done) | data formatting | bytes 8085504
  120.3 20.5 %all-to-all-done = bf16[32,2,7896]{2,1,0:T(2,128)(2,1)} async-done(((bf16[32,2,7896]{2,1,0:T(2,128)(2,1)}), bf16[32,2,7896]{2,1,0:T(2,128)(2,1)}, u32[]{:S(2)}, u32[]{:S(2)}) %all-to-all-start) | async-done | bytes 1010720 | tf_op jit(solution)/shard_map/all_to_all | solution.py:39
  140.9 5.5 %reshape.71 = bf16[1344,8,47]{2,1,0:T(8,128)(2,1)S(1)} reshape(bf16[32,2,7896]{2,1,0:T(2,128)(2,1)} %all-to-all-done) | data formatting | bytes 2021376
  146.4 2.3 copy.51
  148.7 5.7 %reshape.67 = bf16[8,1504,42]{1,2,0:T(8,128)(2,1)S(1)} reshape(bf16[8,32,47,42]{2,1,3,0:T(8,128)(2,1)} %copy.51) | data formatting | bytes 2021376 | tf_op jit(solution)/shard_map/all_to_all | solution.py:39
  154.3 4.2 %convolution_convert_fusion = bf16[8,42,1344]{2,1,0:T(8,128)(2,1)S(1)} fusion(bf16[8,1504,42]{1,2,0:T(8,128)(2,1)S(1)} %reshape.67, bf16[1344,1504,1]{1,0,2:T(8,128)(2,1)} %reshape.65), kind=kOutput, calls=%fused_computation.2 | convolution fusion | flops 1358816256 | bytes 5956608 | tf_op jit(solution)/shard_map/dot_general | solution.py:40
  158.5 8.9 %reshape.69 = bf16[8,42,32,42]{3,2,1,0:T(8,128)(2,1)} reshape(bf16[8,42,1344]{2,1,0:T(8,128)(2,1)S(1)} %convolution_convert_fusion) | data formatting | bytes 1806336 | tf_op jit(solution)/shard_map/reshape | solution.py:46
  167.5 5.0 %copy.44 = bf16[8,42,32,42]{3,0,2,1:T(8,128)(2,1)S(1)} copy(bf16[8,42,32,42]{3,2,1,0:T(8,128)(2,1)} %reshape.69) | data formatting | bytes 1806336 | tf_op jit(solution)/shard_map/reshape | solution.py:46
  172.4 3.0 %gather_fusion = bf16[32,8,42,42]{3,1,2,0:T(8,128)(2,1)} fusion(bf16[8,42,32,42]{3,0,2,1:T(8,128)(2,1)S(1)} %copy.44, s32[1024]{0:T(1024)S(1)} %pad_clamp_fusion.1), kind=kCustom, calls=%fused_computation | custom fusion | bytes 1806464 | tf_op jit(solution)/shard_map/jit(_take)/gather | solution.py:47
  175.4 2.5 %copy.45 = bf16[8,42,32,42]{3,2,1,0:T(8,128)(2,1)S(1)} copy(bf16[8,42,32,42]{3,0,1,2:T(8,128)(2,1)} %bitcast.30) | data formatting | bytes 1806336 | tf_op jit(solution)/shard_map/jit(_take)/gather | solution.py:47
  177.9 2.4 gather.13
  180.3 1.8 fusion
  182.1 0.8 split.8
  182.9 9.5 %all-to-all-start.1 = ((bf16[16,8,16,84]{3,1,2,0:T(8,128)(2,1)}), bf16[16,8,16,84]{3,1,2,0:T(8,128)(2,1)S(1)}, u32[]{:S(2)}, u32[]{:S(2)}) async-start(bf16[16,8,16,84]{3,1,2,0:T(8,128)(2,1)} %split.8), calls=%async_computation.1 | async-start | bytes 1048576 | tf_op jit(solution)/shard_map/all_to_all | solution.py:29
  192.4 0.0 copy-start.1
  192.4 1.0 split.9
  193.4 16.7 %all-to-all-done.1 = bf16[16,8,16,84]{3,1,2,0:T(8,128)(2,1)S(1)} async-done(((bf16[16,8,16,84]{3,1,2,0:T(8,128)(2,1)}), bf16[16,8,16,84]{3,1,2,0:T(8,128)(2,1)S(1)}, u32[]{:S(2)}, u32[]{:S(2)}) %all-to-all-start.1) | async-done | bytes 344096 | tf_op jit(solution)/shard_map/all_to_all | solution.py:29
  210.1 3.6 %all-to-all-start.2 = ((bf16[16,8,26,84]{3,1,2,0:T(8,128)(2,1)}), bf16[16,8,26,84]{3,1,2,0:T(8,128)(2,1)S(1)}, u32[]{:S(2)}, u32[]{:S(2)}) async-start(bf16[16,8,26,84]{3,1,2,0:T(8,128)(2,1)} %split.9), calls=%async_computation.2 | async-start | bytes 1703936 | tf_op jit(solution)/shard_map/all_to_all | solution.py:29
  213.7 0.0 copy-done.1
  213.8 0.2 convert_reduce_fusion
  213.9 0.1 select_reduce_fusion
  214.1 0.1 broadcast_in_dim.37
  214.1 0.1 broadcast_in_dim.38
  214.3 23.0 %all-to-all-done.2 = bf16[16,8,26,84]{3,1,2,0:T(8,128)(2,1)S(1)} async-done(((bf16[16,8,26,84]{3,1,2,0:T(8,128)(2,1)}), bf16[16,8,26,84]{3,1,2,0:T(8,128)(2,1)S(1)}, u32[]{:S(2)}, u32[]{:S(2)}) %all-to-all-start.2) | async-done | bytes 559136 | tf_op jit(solution)/shard_map/all_to_all | solution.py:29
  237.3 0.3 pad_maximum_fusion
  237.6 0.8 gather_fusion.1
  238.4 0.2 bitcast_select_fusion
  238.6 1.5 copy.48
  (6 shorter events, 0.0 us)
Async XLA Ops:
  6.5 76.6 %all-gather.3.cloned.1.call-start = ((), (), s32[]{:S(2)}) async-start(), calls=%async_computation.3 | async-start | bytes 4866048 | tf_op jit(solution)/shard_map/all_gather | solution.py:36
  104.8 7.7 %copy-start = (s32[32]{0:T(128)S(1)}, s32[32]{0:T(128)}, u32[]{:S(2)}) copy-start(s32[32]{0:T(128)} %param.7) | copy-start | bytes 388
  104.8 36.0 %all-to-all-start = ((bf16[32,2,7896]{2,1,0:T(2,128)(2,1)}), bf16[32,2,7896]{2,1,0:T(2,128)(2,1)}, u32[]{:S(2)}, u32[]{:S(2)}) async-start(bf16[32,2,7896]{2,1,0:T(2,128)(2,1)} %reshape.70), calls=%async_computation | async-start | bytes 2031616 | tf_op jit(solution)/shard_map/all_to_all | solution.py:39
  182.9 27.2 %all-to-all-start.1 = ((bf16[16,8,16,84]{3,1,2,0:T(8,128)(2,1)}), bf16[16,8,16,84]{3,1,2,0:T(8,128)(2,1)S(1)}, u32[]{:S(2)}, u32[]{:S(2)}) async-start(bf16[16,8,16,84]{3,1,2,0:T(8,128)(2,1)} %split.8), calls=%async_computation.1 | async-start | bytes 1048576 | tf_op jit(solution)/shard_map/all_to_all | solution.py:29
  192.4 21.3 %copy-start.1 = (s32[16]{0:T(128)S(1)}, s32[16]{0:T(128)}, u32[]{:S(2)}) copy-start(s32[16]{0:T(128)} %param.6) | copy-start | bytes 196
  210.1 27.2 %all-to-all-start.2 = ((bf16[16,8,26,84]{3,1,2,0:T(8,128)(2,1)}), bf16[16,8,26,84]{3,1,2,0:T(8,128)(2,1)S(1)}, u32[]{:S(2)}, u32[]{:S(2)}) async-start(bf16[16,8,26,84]{3,1,2,0:T(8,128)(2,1)} %split.9), calls=%async_computation.2 | async-start | bytes 1703936 | tf_op jit(solution)/shard_map/all_to_all | solution.py:29
Sparse Core Ops, SparseCore 0:
  9.5 73.5 all-gather.2
where the time goes:
time: 248 us; the launch traced here: 247 us
  waiting for transfers between devices  135 us (54%)
  local copies, waits for them, and re-layouts  65.6 us (26%)
  starting transfers between devices  20.8 us (8%)
  between operations  13.6 us (5%)
  matrix products  9.71 us (4%)
  other arithmetic  2.65 us (1%)
    all_gather x1, waiting for transfers between devices, local(): v_whole = lax.all_gather(v_coeff, 'blk', axis=1, tiled=True)  73.7 us
    all_to_all x2, waiting for transfers between devices, several_exchanges(): lax.all_to_all(section, axis, split_axis=0, concat_axis=0, tiled=True)  39.7 us
    unnamed x9, local copies, waits for them, and re-layouts  27 us
    all_to_all x1, waiting for transfers between devices, local(): lax.all_to_all(half_done, 'blk', split_axis=2, concat_axis=1, tiled=True)  20.5 us
    reshape x2, local copies, waits for them, and re-layouts, local(): blocked = third_done.reshape(sig_rows, a_local, block_count, block_width)  13.9 us
    all_to_all x2, starting transfers between devices, several_exchanges(): lax.all_to_all(section, axis, split_axis=0, concat_axis=0, tiled=True)  13.1 us
    all_to_all x2, local copies, waits for them, and re-layouts, local(): lax.all_to_all(half_done, 'blk', split_axis=2, concat_axis=1, tiled=True)  7.93 us
    gather x3, local copies, waits for them, and re-layouts, local(): jnp.take(blocked, owner_map, axis=2)  7.84 us
  transfers between devices with their start and end apart: 4, of which 4 were waited for; matrix products, arithmetic and copies ran while one was open for 5% of the time, Pallas kernels for 0%

commit v1 on v0

--- a/solution.py
+++ b/solution.py
@@ -33,7 +33,9 @@
 def local(ao_ints, v_coeff, batch_start, owner_map):
     sig_rows, lam_rows, ao_count = ao_ints.shape
     ints_flat = ao_ints.reshape(sig_rows * lam_rows, ao_count)
-    v_whole = lax.all_gather(v_coeff, "blk", axis=1, tiled=True)
+    v_whole = jnp.concatenate(
+        lax.all_to_all(jnp.stack([v_coeff] * lax.axis_size("blk")), "blk", 0, 0), axis=1
+    )
     half_done = jnp.dot(ints_flat, v_whole, preferred_element_type=jnp.float32).astype(jnp.bfloat16)
     half_done = half_done.reshape(sig_rows, lam_rows, -1)
     owned_rows = lax.all_to_all(half_done, "blk", split_axis=2, concat_axis=1, tiled=True)

time: 248 us -> 279 us (1.12)
  waiting for transfers between devices: 135 us -> 164 us
  between operations: 13.6 us -> 0.18 us
  starting transfers between devices: 20.8 us -> 33.6 us
    all_to_all x0 -> x1, waiting for transfers between devices: none -> 104 us  [local(): lax.all_to_all(jnp.stack([v_coeff] * lax.axis_size('blk')), 'blk', 0, 0)]
    all_gather x1 -> x0, waiting for transfers between devices: 73.7 us -> none  [local(): v_whole = lax.all_gather(v_coeff, 'blk', axis=1, tiled=True)]
    unnamed x9, local copies, waits for them, and re-layouts: 27 us -> 10.8 us
    reshape x0 -> x2, local copies, waits for them, and re-layouts: none -> 15 us  [local(): jnp.concatenate(lax.all_to_all(jnp.stack([v_coeff] * lax.axis_size('blk')...]
    all_to_all x0 -> x1, starting transfers between devices: none -> 10.4 us  [local(): lax.all_to_all(jnp.stack([v_coeff] * lax.axis_size('blk')), 'blk', 0, 0)]
    another operation x0 -> x1, local copies, waits for them, and re-layouts: none -> 3.6 us  [local(): jnp.stack([v_coeff] * lax.axis_size('blk'))]
  transfers between devices with their start and end apart: 4 -> 4, of which waited for: 4 -> 4; matrix products, arithmetic and copies ran while one was open for 5% -> 4% of each run, Pallas kernels for 0% -> 0%
where the time goes in v1:
time: 279 us; the launch traced here: 278 us
  waiting for transfers between devices  164 us (59%)
  local copies, waits for them, and re-layouts  67.9 us (24%)
  starting transfers between devices  33.6 us (12%)
  matrix products  9.71 us (3%)
    all_to_all x1, waiting for transfers between devices, local(): lax.all_to_all(jnp.stack([v_coeff] * lax.axis_size('blk')), 'blk', 0, 0)  104 us
    all_to_all x2, waiting for transfers between devices, several_exchanges(): lax.all_to_all(section, axis, split_axis=0, concat_axis=0, tiled=True)  39.7 us
    all_to_all x1, waiting for transfers between devices, local(): lax.all_to_all(half_done, 'blk', split_axis=2, concat_axis=1, tiled=True)  20.5 us
    reshape x2, local copies, waits for them, and re-layouts, local(): jnp.concatenate(lax.all_to_all(jnp.stack([v_coeff] * lax.axis_size('blk')...  15 us
    all_to_all x2, starting transfers between devices, several_exchanges(): lax.all_to_all(section, axis, split_axis=0, concat_axis=0, tiled=True)  14.5 us
    reshape x2, local copies, waits for them, and re-layouts, local(): blocked = third_done.reshape(sig_rows, a_local, block_count, block_width)  13.9 us
    unnamed x9, local copies, waits for them, and re-layouts  10.8 us
    all_to_all x1, starting transfers between devices, local(): lax.all_to_all(jnp.stack([v_coeff] * lax.axis_size('blk')), 'blk', 0, 0)  10.4 us
  transfers between devices with their start and end apart: 4, of which 4 were waited for; matrix products, arithmetic and copies ran while one was open for 4% of the time, Pallas kernels for 0%

profile of v1, /device:TPU:8, one launch (start us, length us, event | category | flops | bytes accessed | tf_op | source)
XLA Modules:
  0.0 278.4 jit_solution(2905086653241300545)
XLA Ops:
  0.0 3.6 %stack.2 = bf16[32,1504,42]{1,2,0:T(8,128)(2,1)} broadcast(bf16[1504,42]{0,1:T(8,128)(2,1)} %param.5), dimensions={1,2} | broadcast | bytes 4169088 | tf_op jit(solution)/shard_map/stack | solution.py:37
  3.6 0.0 copy-start
  3.6 10.4 %all-to-all-start = ((bf16[32,1504,42]{1,2,0:T(8,128)(2,1)}), bf16[32,1504,42]{1,2,0:T(8,128)(2,1)}, u32[]{:S(2)}, u32[]{:S(2)}) async-start(bf16[32,1504,42]{1,2,0:T(8,128)(2,1)} %stack.2), calls=%async_computation | async-start | bytes 9437184 | tf_op jit(solution)/shard_map/all_to_all | solution.py:37
  14.0 0.0 copy-done
  14.0 0.3 copy.37
  14.3 0.5 reshape.51
  14.9 104.1 %all-to-all-done = bf16[32,1504,42]{1,2,0:T(8,128)(2,1)} async-done(((bf16[32,1504,42]{1,2,0:T(8,128)(2,1)}), bf16[32,1504,42]{1,2,0:T(8,128)(2,1)}, u32[]{:S(2)}, u32[]{:S(2)}) %all-to-all-start) | async-done | bytes 4042784 | tf_op jit(solution)/shard_map/all_to_all | solution.py:37
  118.9 7.5 %reshape.53 = bf16[1504,1344]{0,1:T(8,128)(2,1)} reshape(bf16[1504,32,42]{0,2,1:T(8,128)(2,1)} %bitcast) | data formatting | bytes 8085504 | tf_op jit(solution)/shard_map/reshape | solution.py:36
  126.4 5.5 %convolution_convert_fusion.1 = bf16[376,1344]{0,1:T(8,128)(2,1)} fusion(bf16[376,1504]{1,0:T(8,128)(2,1)S(1)} %reshape.51, bf16[1504,1344]{0,1:T(8,128)(2,1)} %reshape.53), kind=kOutput, calls=%fused_computation.3 | convolution fusion | flops 1520580096 | bytes 6184448 | tf_op jit(solution)/shard_map/dot_general | solution.py:39
  131.9 3.8 %reshape.74 = bf16[8,47,1344]{1,0,2:T(8,128)(2,1)S(1)} reshape(bf16[376,1344]{0,1:T(8,128)(2,1)} %convolution_convert_fusion.1) | data formatting | bytes 2021376 | tf_op jit(solution)/shard_map/reshape | solution.py:40
  135.8 4.9 %reshape.78 = bf16[32,2,7896]{2,1,0:T(2,128)(2,1)} reshape(bf16[1344,8,47]{2,1,0:T(8,128)(2,1)S(1)} %bitcast.33) | data formatting | bytes 2021376
  140.7 0.0 copy-start.1
  140.7 8.7 %all-to-all-start.1 = ((bf16[32,2,7896]{2,1,0:T(2,128)(2,1)}), bf16[32,2,7896]{2,1,0:T(2,128)(2,1)}, u32[]{:S(2)}, u32[]{:S(2)}) async-start(bf16[32,2,7896]{2,1,0:T(2,128)(2,1)} %reshape.78), calls=%async_computation.1 | async-start | bytes 2031616 | tf_op jit(solution)/shard_map/all_to_all | solution.py:41
  149.4 0.0 copy-done.1
  149.4 0.1 broadcast_in_dim.40
  149.5 0.1 broadcast_in_dim.41
  149.6 0.1 broadcast_in_dim.42
  149.7 7.5 %reshape.73 = bf16[1504,1344,1]{0,1,2:T(8,128)(2,1)} reshape(bf16[1504,32,42]{0,2,1:T(8,128)(2,1)} %bitcast) | data formatting | bytes 8085504 | tf_op jit(solution)/shard_map/reshape | solution.py:36
  157.2 20.5 %all-to-all-done.1 = bf16[32,2,7896]{2,1,0:T(2,128)(2,1)} async-done(((bf16[32,2,7896]{2,1,0:T(2,128)(2,1)}), bf16[32,2,7896]{2,1,0:T(2,128)(2,1)}, u32[]{:S(2)}, u32[]{:S(2)}) %all-to-all-start.1) | async-done | bytes 1010720 | tf_op jit(solution)/shard_map/all_to_all | solution.py:41
  177.7 5.5 %reshape.79 = bf16[1344,8,47]{2,1,0:T(8,128)(2,1)S(1)} reshape(bf16[32,2,7896]{2,1,0:T(2,128)(2,1)} %all-to-all-done.1) | data formatting | bytes 2021376
  183.3 2.3 copy.51
  185.5 5.7 %reshape.75 = bf16[8,1504,42]{1,2,0:T(8,128)(2,1)S(1)} reshape(bf16[8,32,47,42]{2,1,3,0:T(8,128)(2,1)} %copy.51) | data formatting | bytes 2021376 | tf_op jit(solution)/shard_map/all_to_all | solution.py:41
  191.2 4.2 %convolution_convert_fusion = bf16[8,42,1344]{2,1,0:T(8,128)(2,1)S(1)} fusion(bf16[8,1504,42]{1,2,0:T(8,128)(2,1)S(1)} %reshape.75, bf16[1504,1344,1]{0,1,2:T(8,128)(2,1)} %reshape.73), kind=kOutput, calls=%fused_computation.2 | convolution fusion | flops 1358816256 | bytes 5956608 | tf_op jit(solution)/shard_map/dot_general | solution.py:42
  195.4 8.9 %reshape.77 = bf16[8,42,32,42]{3,2,1,0:T(8,128)(2,1)} reshape(bf16[8,42,1344]{2,1,0:T(8,128)(2,1)S(1)} %convolution_convert_fusion) | data formatting | bytes 1806336 | tf_op jit(solution)/shard_map/reshape | solution.py:48
  204.3 5.0 %copy.44 = bf16[8,42,32,42]{3,0,2,1:T(8,128)(2,1)S(1)} copy(bf16[8,42,32,42]{3,2,1,0:T(8,128)(2,1)} %reshape.77) | data formatting | bytes 1806336 | tf_op jit(solution)/shard_map/reshape | solution.py:48
  209.3 3.0 %gather_fusion = bf16[32,8,42,42]{3,1,2,0:T(8,128)(2,1)} fusion(bf16[8,42,32,42]{3,0,2,1:T(8,128)(2,1)S(1)} %copy.44, s32[1024]{0:T(1024)S(1)} %pad_clamp_fusion.1), kind=kCustom, calls=%fused_computation | custom fusion | bytes 1806464 | tf_op jit(solution)/shard_map/jit(_take)/gather | solution.py:49
  212.3 2.5 copy.45
  214.7 2.4 gather.13
  217.1 1.8 fusion
  218.9 0.8 split.8
  219.8 10.9 %all-to-all-start.2 = ((bf16[16,8,16,84]{3,1,2,0:T(8,128)(2,1)}), bf16[16,8,16,84]{3,1,2,0:T(8,128)(2,1)S(1)}, u32[]{:S(2)}, u32[]{:S(2)}) async-start(bf16[16,8,16,84]{3,1,2,0:T(8,128)(2,1)} %split.8), calls=%async_computation.2 | async-start | bytes 1048576 | tf_op jit(solution)/shard_map/all_to_all | solution.py:29
  230.7 0.0 copy-start.2
  230.7 1.0 split.9
  231.7 16.7 %all-to-all-done.2 = bf16[16,8,16,84]{3,1,2,0:T(8,128)(2,1)S(1)} async-done(((bf16[16,8,16,84]{3,1,2,0:T(8,128)(2,1)}), bf16[16,8,16,84]{3,1,2,0:T(8,128)(2,1)S(1)}, u32[]{:S(2)}, u32[]{:S(2)}) %all-to-all-start.2) | async-done | bytes 344096 | tf_op jit(solution)/shard_map/all_to_all | solution.py:29
  248.4 3.6 %all-to-all-start.3 = ((bf16[16,8,26,84]{3,1,2,0:T(8,128)(2,1)}), bf16[16,8,26,84]{3,1,2,0:T(8,128)(2,1)S(1)}, u32[]{:S(2)}, u32[]{:S(2)}) async-start(bf16[16,8,26,84]{3,1,2,0:T(8,128)(2,1)} %split.9), calls=%async_computation.3 | async-start | bytes 1703936 | tf_op jit(solution)/shard_map/all_to_all | solution.py:29
  252.0 0.0 copy-done.2
  252.0 0.2 convert_reduce_fusion
  252.2 0.1 select_reduce_fusion
  252.3 0.1 broadcast_in_dim.37
  252.4 0.1 broadcast_in_dim.38
  252.5 23.0 %all-to-all-done.3 = bf16[16,8,26,84]{3,1,2,0:T(8,128)(2,1)S(1)} async-done(((bf16[16,8,26,84]{3,1,2,0:T(8,128)(2,1)}), bf16[16,8,26,84]{3,1,2,0:T(8,128)(2,1)S(1)}, u32[]{:S(2)}, u32[]{:S(2)}) %all-to-all-start.3) | async-done | bytes 559136 | tf_op jit(solution)/shard_map/all_to_all | solution.py:29
  275.6 0.3 pad_maximum_fusion
  275.8 0.8 gather_fusion.1
  276.6 0.2 bitcast_select_fusion
  276.9 1.5 copy.48
  (6 shorter events, 0.0 us)
Async XLA Ops:
  3.6 10.4 %copy-start = (bf16[8,47,1504]{2,0,1:T(8,128)(2,1)S(1)}, bf16[8,47,1504]{2,0,1:T(8,128)(2,1)}, u32[]{:S(2)}) copy-start(bf16[8,47,1504]{2,0,1:T(8,128)(2,1)} %param.4) | copy-start | bytes 3393028
  3.6 115.3 %all-to-all-start = ((bf16[32,1504,42]{1,2,0:T(8,128)(2,1)}), bf16[32,1504,42]{1,2,0:T(8,128)(2,1)}, u32[]{:S(2)}, u32[]{:S(2)}) async-start(bf16[32,1504,42]{1,2,0:T(8,128)(2,1)} %stack.2), calls=%async_computation | async-start | bytes 9437184 | tf_op jit(solution)/shard_map/all_to_all | solution.py:37
  140.7 8.7 %copy-start.1 = (s32[32]{0:T(128)S(1)}, s32[32]{0:T(128)}, u32[]{:S(2)}) copy-start(s32[32]{0:T(128)} %param.7) | copy-start | bytes 388
  140.7 37.0 %all-to-all-start.1 = ((bf16[32,2,7896]{2,1,0:T(2,128)(2,1)}), bf16[32,2,7896]{2,1,0:T(2,128)(2,1)}, u32[]{:S(2)}, u32[]{:S(2)}) async-start(bf16[32,2,7896]{2,1,0:T(2,128)(2,1)} %reshape.78), calls=%async_computation.1 | async-start | bytes 2031616 | tf_op jit(solution)/shard_map/all_to_all | solution.py:41
  219.8 28.6 %all-to-all-start.2 = ((bf16[16,8,16,84]{3,1,2,0:T(8,128)(2,1)}), bf16[16,8,16,84]{3,1,2,0:T(8,128)(2,1)S(1)}, u32[]{:S(2)}, u32[]{:S(2)}) async-start(bf16[16,8,16,84]{3,1,2,0:T(8,128)(2,1)} %split.8), calls=%async_computation.2 | async-start | bytes 1048576 | tf_op jit(solution)/shard_map/all_to_all | solution.py:29
  230.7 21.3 %copy-start.2 = (s32[16]{0:T(128)S(1)}, s32[16]{0:T(128)}, u32[]{:S(2)}) copy-start(s32[16]{0:T(128)} %param.6) | copy-start | bytes 196
  248.4 27.2 %all-to-all-start.3 = ((bf16[16,8,26,84]{3,1,2,0:T(8,128)(2,1)}), bf16[16,8,26,84]{3,1,2,0:T(8,128)(2,1)S(1)}, u32[]{:S(2)}, u32[]{:S(2)}) async-start(bf16[16,8,26,84]{3,1,2,0:T(8,128)(2,1)} %split.9), calls=%async_computation.3 | async-start | bytes 1703936 | tf_op jit(solution)/shard_map/all_to_all | solution.py:29
